TPU v7x, 32 devices: a whole 2x2x4 slice. The times are simulated.
32 devices in a mesh: rep: 2 (over y), cell: 4 (over z), sub: 4 (over x, core).
Axes of the slice: x: 2, y: 2, z: 4, core: 2. Of those that a mesh axis runs over, the one named last changes fastest.
Arguments:
- descriptors: bfloat16 [8, 4, 128, 128], P(('rep', 'cell'), 'sub'), parts along dimension 0, may hold values from -6 to 6
- positions: float32 [3, 8, 4, 128], P(None, ('rep', 'cell'), 'sub'), parts along dimension 1, may hold values from 0 to 4, as said below
- species: int32 [8, 4, 128], P(('rep', 'cell'), 'sub'), parts along dimension 0, may hold values from 0 to 3
- counts: int32 [8, 4], P(('rep', 'cell'), 'sub'), parts along dimension 0, may hold values from 80 to 128, as said below
- w_in: bfloat16 [8, 128, 256], replicated, may hold values from -0.5 to 0.5
- b_in: float32 [8, 256], replicated, may hold values from -3 to 3
- w_hid: bfloat16 [8, 256, 256], replicated, may hold values from -0.375 to 0.375
- b_hid: float32 [8, 256], replicated, may hold values from -3 to 3
- w_out: bfloat16 [8, 2, 256], replicated, may hold values from -0.375 to 0.375
Outputs:
- charges: float32 [8, 8, 4, 128], P(None, ('rep', 'cell'), 'sub'), parts along dimension 1
There are 2 independent parts, one for each index of `rep`. A program takes and returns all parts, laid end to end along the dimension named above; an argument that names none is the same for every part. Nothing has to cross between parts.
Inputs may be any that keep to these rules, and one draw needn't show every extreme that they name: `positions`: the first two coordinates of a slot lie between its cell's indices and one more, the height between 0 and 1. `counts`: a cell's slots from its count up are empty.
All inputs are finite; a program needn't handle non-finite values.
Results may differ from a plain program's by a relative error of at most 0.0003.
The roundings to bfloat16 on the way count: a program that leaves them out, or rounds other values in their place, can miss the bound.
Values sent between devices are 32-bit elements; how exact they have to be, the bound alone decides.
No kernel may reach another device: no remote copies, remote signals or barrier semaphores. Data moves between devices by JAX's collectives and lax.ppermute only.
A program may use at most 64 MiB of HBM per device.

v0:
```python
import jax
import jax.numpy as jnp
from jax import lax
from jax.sharding import PartitionSpec as P

ITERS = 2


def extended_2(shard, sides, width):
    for axis, dim in sides:
        size, length = (lax.axis_size(axis), shard.shape[dim])
        up = [(i, (i + 1) % size) for i in range(size - 1)]
        down = [(j, i) for i, j in up]
        last = lax.slice_in_dim(shard, length - width, length, axis=dim)
        leading = lax.slice_in_dim(shard, 0, width, axis=dim)
        before = lax.ppermute(last, axis, up)
        after = lax.ppermute(leading, axis, down)
        shard = jnp.concatenate([before, shard, after], axis=dim)
    return shard


def lookup(species, entries):
    choices_table = jnp.array(entries, jnp.float32)
    kinds = jnp.arange(4, dtype=jnp.int32)
    return jnp.sum((species[..., None] == kinds).astype(jnp.float32) * choices_table, axis=-1)


def coupling(own_atoms, far_atoms, self_cell):
    delta_a = own_atoms[0][..., :, None] - far_atoms[0][..., None, :]
    delta_b = own_atoms[1][..., :, None] - far_atoms[1][..., None, :]
    delta_c = own_atoms[2][..., :, None] - far_atoms[2][..., None, :]
    distance_sq = delta_a * delta_a + delta_b * delta_b + delta_c * delta_c
    radius = jnp.sqrt(distance_sq + 1e-06)
    pair_width = jnp.sqrt(own_atoms[3][..., :, None] ** 2 + far_atoms[3][..., None, :] ** 2)
    smooth_cut = (1.0 - jnp.minimum(distance_sq, 1.0)) ** 3
    kernel = 0.005 * smooth_cut * jax.scipy.special.erf(radius / pair_width) / radius
    kernel = kernel * own_atoms[4][..., :, None] * far_atoms[4][..., None, :]
    if self_cell:
        kernel = kernel * (1.0 - jnp.eye(kernel.shape[-1], dtype=jnp.float32))
    return kernel


def committee(flat_rows, w_in, b_in, w_hid, b_hid, w_out):

    def member_fn(weights):
        first_w, first_b, second_w, second_b, last_w = weights
        first = jnp.tanh(
            jnp.dot(flat_rows, first_w, preferred_element_type=jnp.float32) + first_b
        ).astype(jnp.bfloat16)
        second = jnp.tanh(
            jnp.dot(first, second_w, preferred_element_type=jnp.float32) + second_b
        ).astype(jnp.bfloat16)
        return jnp.dot(second, last_w.T, preferred_element_type=jnp.float32).T

    return lax.map(member_fn, (w_in, b_in, w_hid, b_hid, w_out))


def expand(values):
    return values[:, None, None, None]


def extend(vectors):
    return extended_2(vectors, (("cell", 1), ("sub", 2)), 1)


def two_products(residual, image_vec):
    return lax.psum(
        (
            jnp.sum(residual * residual, axis=(1, 2, 3)),
            jnp.sum(residual * image_vec, axis=(1, 2, 3)),
        ),
        ("cell", "sub"),
    )


def body(descriptors, positions, species, counts, w_in, b_in, w_hid, b_hid, w_out):
    rows_a, rows_b, slot_count, features = descriptors.shape
    members = w_in.shape[0]
    slot_iota = lax.broadcasted_iota(jnp.int32, (rows_a, rows_b, slot_count), 2)
    occupancy = (slot_iota < counts[:, :, None]).astype(jnp.float32)
    widths = lookup(species, (0.3, 0.4, 0.5, 0.35))
    shifts = lookup(species, (-0.8, 0.4, 1.2, -0.3))
    atom_data = jnp.stack([positions[0], positions[1], positions[2], widths, occupancy])
    extended = extended_2(atom_data, (("cell", 1), ("sub", 2)), 1)
    outputs = committee(descriptors.reshape(-1, features), w_in, b_in, w_hid, b_hid, w_out)
    electro = outputs[:, 0].reshape(members, rows_a, rows_b, slot_count) + shifts
    hardness = 2.5 + jax.nn.softplus(outputs[:, 1]).reshape(members, rows_a, rows_b, slot_count)
    right_side = jnp.concatenate([-electro * occupancy, jnp.broadcast_to(occupancy, electro.shape)])
    diagonal = jnp.concatenate([hardness, hardness])
    offsets = [(row_step, col_step) for row_step in (-1, 0, 1) for col_step in (-1, 0, 1)]

    def neighbours(grown, row_step, col_step):
        return grown[:, 1 + row_step : 1 + row_step + rows_a, 1 + col_step : 1 + col_step + rows_b]

    def block_for(row_step, col_step):
        return coupling(
            atom_data, neighbours(extended, row_step, col_step), row_step == 0 and col_step == 0
        )

    def operate(vectors):
        grown = extend(vectors)
        summed = diagonal * vectors
        for offset_number in range(9):
            row_step, col_step = offsets[offset_number]
            tile_block = block_for(row_step, col_step)
            summed = summed + jnp.einsum(
                "abij,rabj->rabi",
                tile_block,
                neighbours(grown, row_step, col_step),
                precision=lax.Precision.HIGHEST,
            )
        return summed

    solution = jnp.zeros_like(right_side)
    residual = right_side
    image_vec = operate(residual)
    norm_now, product = two_products(residual, image_vec)
    step_size = norm_now / product
    direction = residual
    along = image_vec
    for iteration in range(ITERS):
        solution = solution + expand(step_size) * direction
        residual = residual - expand(step_size) * along
        if iteration + 1 < ITERS:
            image_vec = operate(residual)
            norm_next, product = two_products(residual, image_vec)
            momentum = norm_next / norm_now
            step_size = norm_next / (product - momentum * norm_next / step_size)
            direction = residual + expand(momentum) * direction
            along = image_vec + expand(momentum) * along
            norm_now = norm_next
    source_part = solution[:members]
    unit_part = solution[members:]
    source_total, unit_total = lax.psum(
        (jnp.sum(source_part, axis=(1, 2, 3)), jnp.sum(unit_part, axis=(1, 2, 3))), ("cell", "sub")
    )
    multiplier = source_total / unit_total
    return source_part - expand(multiplier) * unit_part


def solution(mesh):
    placed = (
        P(("rep", "cell"), "sub", None, None),
        P(None, ("rep", "cell"), "sub", None),
        P(("rep", "cell"), "sub", None),
        P(("rep", "cell"), "sub"),
        P(),
        P(),
        P(),
        P(),
        P(),
    )
    return jax.shard_map(
        body,
        mesh=mesh,
        in_specs=placed,
        out_specs=P(None, ("rep", "cell"), "sub", None),
        check_vma=False,
    )
```

profile of v0, /device:TPU:0, one launch (start us, length us, event | category | flops | bytes accessed | tf_op | source)
XLA Modules:
  0.0 162.4 jit_solution(817328596570709719)
XLA Ops:
  0.7 24.5 %while.10 = (s32[]{:T(128)}, f32[8,2,128]{2,0,1:T(8,128)S(1)}, bf16[8,2,256]{2,1,0:T(2,128)(2,1)}, bf16[8,128,256]{2,1,0:T(8,128)(2,1)}, bf16[128,128]{1,0:T(8,1...) while((s32[]{:T(128)}, f32[8,2,128]{2,0,1:T(8,128)S(1)}, ...), condition=%wide.region_1.0_spmd, body=%wide.region_0.0_spmd.sunk | while | flops 25427968 | bytes 372333 | solution.py:55
  5.5 1.2 fusion.171
  8.6 1.2 fusion.171
  11.6 1.2 fusion.171
  14.7 1.2 fusion.171
  17.7 1.2 fusion.171
  20.8 1.2 fusion.171
  26.1 4.9 %collective-permute-start = (f32[16,1,1,128]{3,0,2,1:T(8,128)S(1)}, f32[16,1,1,128]{3,0,2,1:T(8,128)S(1)}, u32[]{:S(2)}, u32[]{:S(2)}) collective-permute-start(f32[16,1,1,128]{3,0,2,1:T(8,128)S(1)} %get-tuple-element.113), channel_id=1, source_target_pairs={{0,4},{4,8},{8,12},{1,5},{5,9},{9,13},{2,6},{6,10},{10,14},{3,7},{... | collective-permute-start | bytes 24584 | tf_op jit(solution)/shard_map/ppermute | solution.py:16
  31.0 1.3 collective-permute-start.1
  33.0 4.5 %collective-permute-start.3 = (f32[5,1,1,128]{3,2,1,0:T(1,128)S(1)}, f32[5,1,1,128]{3,2,1,0:T(1,128)S(1)}, u32[]{:S(2)}, u32[]{:S(2)}) collective-permute-start(f32[5,1,1,128]{3,2,1,0:T(1,128)S(1)} %pad_maximum_fusion.7), channel_id=1, source_target_pairs={{0,4},{4,8},{8,12},{1,5},{5,9},{9,13},{2,6},{6,10},{10,14},{3,7},{... | collective-permute-start | bytes 7688 | tf_op jit(solution)/shard_map/ppermute | solution.py:16
  37.5 1.3 collective-permute-start.4
  39.2 3.8 %collective-permute-done.4 = f32[5,1,1,128]{3,2,1,0:T(1,128)S(1)} collective-permute-done((f32[5,1,1,128]{3,2,1,0:T(1,128)S(1)}, f32[5,1,1,128]{3,2,1,0:T(1,128)S(1)}, u32[]{:S(2)}, u32[]{:S(2)}) %collective-permute-start.4) | collective-permute-done | bytes 2592 | tf_op jit(solution)/shard_map/ppermute | solution.py:17
  43.0 1.3 collective-permute-start.7
  44.3 3.0 %collective-permute-start.5 = (f32[5,3,1,128]{3,2,1,0:T(1,128)S(1)}, f32[5,3,1,128]{3,2,1,0:T(1,128)S(1)}, u32[]{:S(2)}, u32[]{:S(2)}) collective-permute-start(f32[5,3,1,128]{3,2,1,0:T(1,128)S(1)} %pad_maximum_fusion.6), channel_id=1, source_target_pairs={{0,1},{1,2},{2,3},{4,5},{5,6},{6,7},{8,9},{9,10},{10,11},{12,13},{... | collective-permute-start | bytes 23048 | tf_op jit(solution)/shard_map/ppermute | solution.py:16
  47.4 1.3 collective-permute-start.6
  48.7 3.6 %collective-permute-start.2 = (f32[16,3,1,128]{3,0,2,1:T(8,128)S(1)}, f32[16,3,1,128]{3,0,2,1:T(8,128)S(1)}, u32[]{:S(2)}, u32[]{:S(2)}) collective-permute-start(f32[16,3,1,128]{3,0,2,1:T(8,128)S(1)} %pad_maximum_fusion), channel_id=1, source_target_pairs={{0,1},{1,2},{2,3},{4,5},{5,6},{6,7},{8,9},{9,10},{10,11},{12,13},{... | collective-permute-start | bytes 73736 | tf_op jit(solution)/shard_map/ppermute | solution.py:16
  55.5 32.3 %all-reduce.2 = (f32[16]{0:T(128)S(1)}, f32[16]{0:T(128)S(1)}) all-reduce(f32[16]{0:T(128)S(1)} %get-tuple-element.112, f32[16]{0:T(128)S(1)} %get-tuple-element.127), channel_id=1, replica_groups=mesh['rep'=2,'cell'=4,'sub'=4] {'cell','sub'}, use_global_device_ids=true, to_apply=%region_4.5 | all-reduce | flops 32 | bytes 256 | tf_op jit(solution)/shard_map/psum | solution.py:67
  87.9 1.3 collective-permute-start.8
  89.2 1.3 collective-permute-start.9
  90.9 3.9 %collective-permute-done.9 = f32[16,1,1,128]{3,0,2,1:T(8,128)S(1)} collective-permute-done((f32[16,1,1,128]{3,0,2,1:T(8,128)S(1)}, f32[16,1,1,128]{3,0,2,1:T(8,128)S(1)}, u32[]{:S(2)}, u32[]{:S(2)}) %collective-permute-start.9) | collective-permute-done | bytes 8224 | tf_op jit(solution)/shard_map/ppermute | solution.py:17
  94.8 1.3 collective-permute-start.11
  96.1 3.0 %collective-permute-start.10 = (f32[16,3,1,128]{3,0,2,1:T(8,128)S(1)}, f32[16,3,1,128]{3,0,2,1:T(8,128)S(1)}, u32[]{:S(2)}, u32[]{:S(2)}) collective-permute-start(f32[16,3,1,128]{3,0,2,1:T(8,128)S(1)} %pad_maximum_fusion.1), channel_id=1, source_target_pairs={{0,1},{1,2},{2,3},{4,5},{5,6},{6,7},{8,9},{9,10},{10,11},{12,13},{... | collective-permute-start | bytes 73736 | tf_op jit(solution)/shard_map/ppermute | solution.py:16
  102.2 29.8 %all-reduce.1 = (f32[16]{0:T(128)S(1)}, f32[16]{0:T(128)S(1)}) all-reduce(f32[16]{0:T(128)S(1)} %get-tuple-element.76, f32[16]{0:T(128)S(1)} %fusion.32), channel_id=1, replica_groups=mesh['rep'=2,'cell'=4,'sub'=4] {'cell','sub'}, use_global_device_ids=true, to_apply=%region_9.10 | all-reduce | flops 32 | bytes 256 | tf_op jit(solution)/shard_map/psum | solution.py:67
  132.3 29.5 %all-reduce = (f32[8]{0:T(128)S(1)}, f32[8]{0:T(128)S(1)}) all-reduce(f32[8]{0:T(128)S(1)} %get-tuple-element.49, f32[8]{0:T(128)S(1)} %get-tuple-element.48), channel_id=1, replica_groups=mesh['rep'=2,'cell'=4,'sub'=4] {'cell','sub'}, use_global_device_ids=true, to_apply=%region_13.14 | all-reduce | flops 16 | bytes 128 | tf_op jit(solution)/shard_map/psum | solution.py:134
  (88 shorter events, 26.3 us)
Async XLA Ops:
  25.1 0.7 copy-start.1
  25.1 0.7 copy-start.2
  25.1 0.7 copy-start.3
  26.1 21.3 %collective-permute-start = (f32[16,1,1,128]{3,0,2,1:T(8,128)S(1)}, f32[16,1,1,128]{3,0,2,1:T(8,128)S(1)}, u32[]{:S(2)}, u32[]{:S(2)}) collective-permute-start(f32[16,1,1,128]{3,0,2,1:T(8,128)S(1)} %get-tuple-element.113), channel_id=1, source_target_pairs={{0,4},{4,8},{8,12},{1,5},{5,9},{9,13},{2,6},{6,10},{10,14},{3,7},{... | collective-permute-start | bytes 24584 | tf_op jit(solution)/shard_map/ppermute | solution.py:16
  31.0 16.4 %collective-permute-start.1 = (f32[16,1,1,128]{3,0,2,1:T(8,128)S(1)}, f32[16,1,1,128]{3,0,2,1:T(8,128)S(1)}, u32[]{:S(2)}, u32[]{:S(2)}) collective-permute-start(f32[16,1,1,128]{3,0,2,1:T(8,128)S(1)} %get-tuple-element.113), channel_id=1, source_target_pairs={{4,0},{8,4},{12,8},{5,1},{9,5},{13,9},{6,2},{10,6},{14,10},{7,3},{... | collective-permute-start | bytes 24584 | tf_op jit(solution)/shard_map/ppermute | solution.py:17
  32.3 0.7 copy-start
  33.0 6.2 %collective-permute-start.3 = (f32[5,1,1,128]{3,2,1,0:T(1,128)S(1)}, f32[5,1,1,128]{3,2,1,0:T(1,128)S(1)}, u32[]{:S(2)}, u32[]{:S(2)}) collective-permute-start(f32[5,1,1,128]{3,2,1,0:T(1,128)S(1)} %pad_maximum_fusion.7), channel_id=1, source_target_pairs={{0,4},{4,8},{8,12},{1,5},{5,9},{9,13},{2,6},{6,10},{10,14},{3,7},{... | collective-permute-start | bytes 7688 | tf_op jit(solution)/shard_map/ppermute | solution.py:16
  37.5 5.5 %collective-permute-start.4 = (f32[5,1,1,128]{3,2,1,0:T(1,128)S(1)}, f32[5,1,1,128]{3,2,1,0:T(1,128)S(1)}, u32[]{:S(2)}, u32[]{:S(2)}) collective-permute-start(f32[5,1,1,128]{3,2,1,0:T(1,128)S(1)} %pad_maximum_fusion.7), channel_id=1, source_target_pairs={{4,0},{8,4},{12,8},{5,1},{9,5},{13,9},{6,2},{10,6},{14,10},{7,3},{... | collective-permute-start | bytes 7688 | tf_op jit(solution)/shard_map/ppermute | solution.py:17
  43.0 10.0 %collective-permute-start.7 = (f32[5,3,1,128]{3,2,1,0:T(1,128)S(1)}, f32[5,3,1,128]{3,2,1,0:T(1,128)S(1)}, u32[]{:S(2)}, u32[]{:S(2)}) collective-permute-start(f32[5,3,1,128]{3,2,1,0:T(1,128)S(1)} %pad_maximum_fusion.6), channel_id=1, source_target_pairs={{1,0},{2,1},{3,2},{5,4},{6,5},{7,6},{9,8},{10,9},{11,10},{13,12},{... | collective-permute-start | bytes 23048 | tf_op jit(solution)/shard_map/ppermute | solution.py:17
  44.3 8.8 %collective-permute-start.5 = (f32[5,3,1,128]{3,2,1,0:T(1,128)S(1)}, f32[5,3,1,128]{3,2,1,0:T(1,128)S(1)}, u32[]{:S(2)}, u32[]{:S(2)}) collective-permute-start(f32[5,3,1,128]{3,2,1,0:T(1,128)S(1)} %pad_maximum_fusion.6), channel_id=1, source_target_pairs={{0,1},{1,2},{2,3},{4,5},{5,6},{6,7},{8,9},{9,10},{10,11},{12,13},{... | collective-permute-start | bytes 23048 | tf_op jit(solution)/shard_map/ppermute | solution.py:16
  47.4 6.5 %collective-permute-start.6 = (f32[16,3,1,128]{3,0,2,1:T(8,128)S(1)}, f32[16,3,1,128]{3,0,2,1:T(8,128)S(1)}, u32[]{:S(2)}, u32[]{:S(2)}) collective-permute-start(f32[16,3,1,128]{3,0,2,1:T(8,128)S(1)} %pad_maximum_fusion), channel_id=1, source_target_pairs={{1,0},{2,1},{3,2},{5,4},{6,5},{7,6},{9,8},{10,9},{11,10},{13,12},{... | collective-permute-start | bytes 73736 | tf_op jit(solution)/shard_map/ppermute | solution.py:17
  48.7 4.5 %collective-permute-start.2 = (f32[16,3,1,128]{3,0,2,1:T(8,128)S(1)}, f32[16,3,1,128]{3,0,2,1:T(8,128)S(1)}, u32[]{:S(2)}, u32[]{:S(2)}) collective-permute-start(f32[16,3,1,128]{3,0,2,1:T(8,128)S(1)} %pad_maximum_fusion), channel_id=1, source_target_pairs={{0,1},{1,2},{2,3},{4,5},{5,6},{6,7},{8,9},{9,10},{10,11},{12,13},{... | collective-permute-start | bytes 73736 | tf_op jit(solution)/shard_map/ppermute | solution.py:16
  87.9 2.9 %collective-permute-start.8 = (f32[16,1,1,128]{3,0,2,1:T(8,128)S(1)}, f32[16,1,1,128]{3,0,2,1:T(8,128)S(1)}, u32[]{:S(2)}, u32[]{:S(2)}) collective-permute-start(f32[16,1,1,128]{3,0,2,1:T(8,128)S(1)} %bitcast.216), channel_id=1, source_target_pairs={{0,4},{4,8},{8,12},{1,5},{5,9},{9,13},{2,6},{6,10},{10,14},{3,7},{... | collective-permute-start | bytes 24584 | tf_op jit(solution)/shard_map/ppermute | solution.py:16
  89.2 5.5 %collective-permute-start.9 = (f32[16,1,1,128]{3,0,2,1:T(8,128)S(1)}, f32[16,1,1,128]{3,0,2,1:T(8,128)S(1)}, u32[]{:S(2)}, u32[]{:S(2)}) collective-permute-start(f32[16,1,1,128]{3,0,2,1:T(8,128)S(1)} %bitcast.217), channel_id=1, source_target_pairs={{4,0},{8,4},{12,8},{5,1},{9,5},{13,9},{6,2},{10,6},{14,10},{7,3},{... | collective-permute-start | bytes 24584 | tf_op jit(solution)/shard_map/ppermute | solution.py:17
  94.8 5.8 %collective-permute-start.11 = (f32[16,3,1,128]{3,0,2,1:T(8,128)S(1)}, f32[16,3,1,128]{3,0,2,1:T(8,128)S(1)}, u32[]{:S(2)}, u32[]{:S(2)}) collective-permute-start(f32[16,3,1,128]{3,0,2,1:T(8,128)S(1)} %pad_maximum_fusion.1), channel_id=1, source_target_pairs={{1,0},{2,1},{3,2},{5,4},{6,5},{7,6},{9,8},{10,9},{11,10},{13,12},{... | collective-permute-start | bytes 73736 | tf_op jit(solution)/shard_map/ppermute | solution.py:17
  96.1 3.9 %collective-permute-start.10 = (f32[16,3,1,128]{3,0,2,1:T(8,128)S(1)}, f32[16,3,1,128]{3,0,2,1:T(8,128)S(1)}, u32[]{:S(2)}, u32[]{:S(2)}) collective-permute-start(f32[16,3,1,128]{3,0,2,1:T(8,128)S(1)} %pad_maximum_fusion.1), channel_id=1, source_target_pairs={{0,1},{1,2},{2,3},{4,5},{5,6},{6,7},{8,9},{9,10},{10,11},{12,13},{... | collective-permute-start | bytes 73736 | tf_op jit(solution)/shard_map/ppermute | solution.py:16
where the time goes:
time: 164 us; the launch traced here: 162 us
  blocking collectives  91.6 us (56%)
  starting transfers between devices  28.2 us (17%)
  matrix products  24.6 us (15%)
  waiting for transfers between devices  8.07 us (5%)
  local copies, waits for them, and re-layouts  7.33 us (4%)
    psum x2, blocking collectives, two_products(): lax.psum((jnp.sum(residual * residual, axis=(1, 2, 3)), jnp.sum(residual...  62.1 us
    psum x1, blocking collectives, body(): lax.psum((jnp.sum(source_part, axis=(1, 2, 3)), jnp.sum(unit_part, axis=(...  29.5 us
    ppermute x6, starting transfers between devices, extended_2(): before = lax.ppermute(last, axis, up)  20.5 us
    dot_general x8, matrix products, member_fn(): return jnp.dot(second, last_w.T, preferred_element_type=jnp.float32).T  9.96 us
    dot_general x8, matrix products, member_fn(): jnp.dot(flat_rows, first_w, preferred_element_type=jnp.float32) + first_b  8.33 us
    ppermute x6, waiting for transfers between devices, extended_2(): after = lax.ppermute(leading, axis, down)  7.78 us
    ppermute x6, starting transfers between devices, extended_2(): after = lax.ppermute(leading, axis, down)  7.74 us
    dot_general x18, matrix products, operate(): jnp.einsum('abij,rabj->rabi', tile_block, neighbours(grown, row_step, col...  6.36 us
  transfers between devices with their start and end apart: 12, of which 4 were waited for; matrix products, arithmetic and copies ran while one was open for 2% of the time, Pallas kernels for 0%

commit v1 on v0

--- a/solution.py
+++ b/solution.py
@@ -1,9 +1,20 @@
+import functools
 import jax
 import jax.numpy as jnp
 from jax import lax
 from jax.sharding import PartitionSpec as P
+from jax.lax import psum
 
 ITERS = 2
+
+
+def process_samples_all_on_mesh(piece_in, named_axis, ax_name):
+    return psum(psum(piece_in, named_axis), ax_name)
+
+
+search_leaf_by_axis = functools.partial(
+    process_samples_all_on_mesh, named_axis="sub", ax_name="cell"
+)
 
 
 def extended_2(shard, sides, width):
@@ -131,8 +142,8 @@
             norm_now = norm_next
     source_part = solution[:members]
     unit_part = solution[members:]
-    source_total, unit_total = lax.psum(
-        (jnp.sum(source_part, axis=(1, 2, 3)), jnp.sum(unit_part, axis=(1, 2, 3))), ("cell", "sub")
+    source_total, unit_total = search_leaf_by_axis(
+        (jnp.sum(source_part, axis=(1, 2, 3)), jnp.sum(unit_part, axis=(1, 2, 3)))
     )
     multiplier = source_total / unit_total
     return source_part - expand(multiplier) * unit_part

time: 164 us -> 149 us (0.909)
  blocking collectives: 91.6 us -> 76.2 us
    psum x1 -> x2, blocking collectives: 29.5 us -> 14.1 us  [process_samples_all_on_mesh(): return psum(psum(piece_in, named_axis), ax_name)]
where the time goes in v1:
time: 149 us; the launch traced here: 147 us
  blocking collectives  76.2 us (51%)
  starting transfers between devices  28.2 us (19%)
  matrix products  24.6 us (17%)
  waiting for transfers between devices  8.07 us (5%)
  local copies, waits for them, and re-layouts  7.33 us (5%)
    psum x2, blocking collectives, two_products(): lax.psum((jnp.sum(residual * residual, axis=(1, 2, 3)), jnp.sum(residual...  62.1 us
    ppermute x6, starting transfers between devices, extended_2(): before = lax.ppermute(last, axis, up)  20.5 us
    psum x2, blocking collectives, process_samples_all_on_mesh(): return psum(psum(piece_in, named_axis), ax_name)  14.1 us
    dot_general x8, matrix products, member_fn(): return jnp.dot(second, last_w.T, preferred_element_type=jnp.float32).T  9.96 us
    dot_general x8, matrix products, member_fn(): jnp.dot(flat_rows, first_w, preferred_element_type=jnp.float32) + first_b  8.33 us
    ppermute x6, waiting for transfers between devices, extended_2(): after = lax.ppermute(leading, axis, down)  7.78 us
    ppermute x6, starting transfers between devices, extended_2(): after = lax.ppermute(leading, axis, down)  7.74 us
    dot_general x18, matrix products, operate(): jnp.einsum('abij,rabj->rabi', tile_block, neighbours(grown, row_step, col...  6.36 us
  transfers between devices with their start and end apart: 12, of which 4 were waited for; matrix products, arithmetic and copies ran while one was open for 2% of the time, Pallas kernels for 0%

profile of v1, /device:TPU:0, one launch (start us, length us, event | category | flops | bytes accessed | tf_op | source)
XLA Modules:
  0.0 147.0 jit_solution(10411510981948046390)
XLA Ops:
  0.7 24.5 %while.10 = (s32[]{:T(128)}, f32[8,2,128]{2,0,1:T(8,128)S(1)}, bf16[8,2,256]{2,1,0:T(2,128)(2,1)}, bf16[8,128,256]{2,1,0:T(8,128)(2,1)}, bf16[128,128]{1,0:T(8,1...) while((s32[]{:T(128)}, f32[8,2,128]{2,0,1:T(8,128)S(1)}, ...), condition=%wide.region_1.0_spmd, body=%wide.region_0.0_spmd.sunk | while | flops 25427968 | bytes 372333 | solution.py:66
  8.6 1.2 fusion.171
  11.6 1.2 fusion.171
  14.7 1.2 fusion.171
  17.7 1.2 fusion.171
  20.8 1.2 fusion.171
  26.1 4.9 %collective-permute-start = (f32[16,1,1,128]{3,0,2,1:T(8,128)S(1)}, f32[16,1,1,128]{3,0,2,1:T(8,128)S(1)}, u32[]{:S(2)}, u32[]{:S(2)}) collective-permute-start(f32[16,1,1,128]{3,0,2,1:T(8,128)S(1)} %get-tuple-element.115), channel_id=1, source_target_pairs={{0,4},{4,8},{8,12},{1,5},{5,9},{9,13},{2,6},{6,10},{10,14},{3,7},{... | collective-permute-start | bytes 24584 | tf_op jit(solution)/shard_map/ppermute | solution.py:27
  31.0 1.3 collective-permute-start.1
  33.0 4.5 %collective-permute-start.3 = (f32[5,1,1,128]{3,2,1,0:T(1,128)S(1)}, f32[5,1,1,128]{3,2,1,0:T(1,128)S(1)}, u32[]{:S(2)}, u32[]{:S(2)}) collective-permute-start(f32[5,1,1,128]{3,2,1,0:T(1,128)S(1)} %pad_maximum_fusion.7), channel_id=1, source_target_pairs={{0,4},{4,8},{8,12},{1,5},{5,9},{9,13},{2,6},{6,10},{10,14},{3,7},{... | collective-permute-start | bytes 7688 | tf_op jit(solution)/shard_map/ppermute | solution.py:27
  37.5 1.3 collective-permute-start.4
  39.2 3.8 %collective-permute-done.4 = f32[5,1,1,128]{3,2,1,0:T(1,128)S(1)} collective-permute-done((f32[5,1,1,128]{3,2,1,0:T(1,128)S(1)}, f32[5,1,1,128]{3,2,1,0:T(1,128)S(1)}, u32[]{:S(2)}, u32[]{:S(2)}) %collective-permute-start.4) | collective-permute-done | bytes 2592 | tf_op jit(solution)/shard_map/ppermute | solution.py:28
  43.0 1.3 collective-permute-start.7
  44.3 3.0 %collective-permute-start.5 = (f32[5,3,1,128]{3,2,1,0:T(1,128)S(1)}, f32[5,3,1,128]{3,2,1,0:T(1,128)S(1)}, u32[]{:S(2)}, u32[]{:S(2)}) collective-permute-start(f32[5,3,1,128]{3,2,1,0:T(1,128)S(1)} %pad_maximum_fusion.6), channel_id=1, source_target_pairs={{0,1},{1,2},{2,3},{4,5},{5,6},{6,7},{8,9},{9,10},{10,11},{12,13},{... | collective-permute-start | bytes 23048 | tf_op jit(solution)/shard_map/ppermute | solution.py:27
  47.4 1.3 collective-permute-start.6
  48.7 3.6 %collective-permute-start.2 = (f32[16,3,1,128]{3,0,2,1:T(8,128)S(1)}, f32[16,3,1,128]{3,0,2,1:T(8,128)S(1)}, u32[]{:S(2)}, u32[]{:S(2)}) collective-permute-start(f32[16,3,1,128]{3,0,2,1:T(8,128)S(1)} %pad_maximum_fusion), channel_id=1, source_target_pairs={{0,1},{1,2},{2,3},{4,5},{5,6},{6,7},{8,9},{9,10},{10,11},{12,13},{... | collective-permute-start | bytes 73736 | tf_op jit(solution)/shard_map/ppermute | solution.py:27
  55.5 32.3 %all-reduce.1 = (f32[16]{0:T(128)S(1)}, f32[16]{0:T(128)S(1)}) all-reduce(f32[16]{0:T(128)S(1)} %get-tuple-element.114, f32[16]{0:T(128)S(1)} %get-tuple-element.129), channel_id=1, replica_groups=mesh['rep'=2,'cell'=4,'sub'=4] {'cell','sub'}, use_global_device_ids=true, to_apply=%region_4.5 | all-reduce | flops 32 | bytes 256 | tf_op jit(solution)/shard_map/psum | solution.py:78
  87.9 1.3 collective-permute-start.8
  89.2 1.3 collective-permute-start.9
  90.9 3.9 %collective-permute-done.9 = f32[16,1,1,128]{3,0,2,1:T(8,128)S(1)} collective-permute-done((f32[16,1,1,128]{3,0,2,1:T(8,128)S(1)}, f32[16,1,1,128]{3,0,2,1:T(8,128)S(1)}, u32[]{:S(2)}, u32[]{:S(2)}) %collective-permute-start.9) | collective-permute-done | bytes 8224 | tf_op jit(solution)/shard_map/ppermute | solution.py:28
  94.8 1.3 collective-permute-start.11
  96.1 3.0 %collective-permute-start.10 = (f32[16,3,1,128]{3,0,2,1:T(8,128)S(1)}, f32[16,3,1,128]{3,0,2,1:T(8,128)S(1)}, u32[]{:S(2)}, u32[]{:S(2)}) collective-permute-start(f32[16,3,1,128]{3,0,2,1:T(8,128)S(1)} %pad_maximum_fusion.1), channel_id=1, source_target_pairs={{0,1},{1,2},{2,3},{4,5},{5,6},{6,7},{8,9},{9,10},{10,11},{12,13},{... | collective-permute-start | bytes 73736 | tf_op jit(solution)/shard_map/ppermute | solution.py:27
  102.2 29.8 %all-reduce = (f32[16]{0:T(128)S(1)}, f32[16]{0:T(128)S(1)}) all-reduce(f32[16]{0:T(128)S(1)} %get-tuple-element.78, f32[16]{0:T(128)S(1)} %fusion.32), channel_id=1, replica_groups=mesh['rep'=2,'cell'=4,'sub'=4] {'cell','sub'}, use_global_device_ids=true, to_apply=%region_9.10 | all-reduce | flops 32 | bytes 256 | tf_op jit(solution)/shard_map/psum | solution.py:78
  132.3 5.8 %all-reduce.2 = (f32[8]{0:T(128)S(1)}, f32[8]{0:T(128)S(1)}) all-reduce(f32[8]{0:T(128)S(1)} %get-tuple-element.49, f32[8]{0:T(128)S(1)} %get-tuple-element.48), channel_id=1, replica_groups=mesh['rep'=2,'cell'=4,'sub'=4] {'sub'}, use_global_device_ids=true, to_apply=%region_13.14 | all-reduce | flops 16 | bytes 128 | tf_op jit(solution)/shard_map/psum | solution.py:12
  138.0 8.4 %all-reduce.3 = (f32[8]{0:T(128)S(1)}, f32[8]{0:T(128)S(1)}) all-reduce(f32[8]{0:T(128)S(1)} %get-tuple-element.72, f32[8]{0:T(128)S(1)} %get-tuple-element.73), channel_id=1, replica_groups=mesh['rep'=2,'cell'=4,'sub'=4] {'cell'}, use_global_device_ids=true, to_apply=%region_14.15 | all-reduce | flops 16 | bytes 128 | tf_op jit(solution)/shard_map/psum | solution.py:12
  (89 shorter events, 27.5 us)
Async XLA Ops:
  25.1 0.7 copy-start.1
  25.1 0.7 copy-start.2
  25.1 0.7 copy-start.3
  26.1 21.3 %collective-permute-start = (f32[16,1,1,128]{3,0,2,1:T(8,128)S(1)}, f32[16,1,1,128]{3,0,2,1:T(8,128)S(1)}, u32[]{:S(2)}, u32[]{:S(2)}) collective-permute-start(f32[16,1,1,128]{3,0,2,1:T(8,128)S(1)} %get-tuple-element.115), channel_id=1, source_target_pairs={{0,4},{4,8},{8,12},{1,5},{5,9},{9,13},{2,6},{6,10},{10,14},{3,7},{... | collective-permute-start | bytes 24584 | tf_op jit(solution)/shard_map/ppermute | solution.py:27
  31.0 16.4 %collective-permute-start.1 = (f32[16,1,1,128]{3,0,2,1:T(8,128)S(1)}, f32[16,1,1,128]{3,0,2,1:T(8,128)S(1)}, u32[]{:S(2)}, u32[]{:S(2)}) collective-permute-start(f32[16,1,1,128]{3,0,2,1:T(8,128)S(1)} %get-tuple-element.115), channel_id=1, source_target_pairs={{4,0},{8,4},{12,8},{5,1},{9,5},{13,9},{6,2},{10,6},{14,10},{7,3},{... | collective-permute-start | bytes 24584 | tf_op jit(solution)/shard_map/ppermute | solution.py:28
  32.3 0.7 copy-start
  33.0 6.2 %collective-permute-start.3 = (f32[5,1,1,128]{3,2,1,0:T(1,128)S(1)}, f32[5,1,1,128]{3,2,1,0:T(1,128)S(1)}, u32[]{:S(2)}, u32[]{:S(2)}) collective-permute-start(f32[5,1,1,128]{3,2,1,0:T(1,128)S(1)} %pad_maximum_fusion.7), channel_id=1, source_target_pairs={{0,4},{4,8},{8,12},{1,5},{5,9},{9,13},{2,6},{6,10},{10,14},{3,7},{... | collective-permute-start | bytes 7688 | tf_op jit(solution)/shard_map/ppermute | solution.py:27
  37.5 5.5 %collective-permute-start.4 = (f32[5,1,1,128]{3,2,1,0:T(1,128)S(1)}, f32[5,1,1,128]{3,2,1,0:T(1,128)S(1)}, u32[]{:S(2)}, u32[]{:S(2)}) collective-permute-start(f32[5,1,1,128]{3,2,1,0:T(1,128)S(1)} %pad_maximum_fusion.7), channel_id=1, source_target_pairs={{4,0},{8,4},{12,8},{5,1},{9,5},{13,9},{6,2},{10,6},{14,10},{7,3},{... | collective-permute-start | bytes 7688 | tf_op jit(solution)/shard_map/ppermute | solution.py:28
  43.0 10.0 %collective-permute-start.7 = (f32[5,3,1,128]{3,2,1,0:T(1,128)S(1)}, f32[5,3,1,128]{3,2,1,0:T(1,128)S(1)}, u32[]{:S(2)}, u32[]{:S(2)}) collective-permute-start(f32[5,3,1,128]{3,2,1,0:T(1,128)S(1)} %pad_maximum_fusion.6), channel_id=1, source_target_pairs={{1,0},{2,1},{3,2},{5,4},{6,5},{7,6},{9,8},{10,9},{11,10},{13,12},{... | collective-permute-start | bytes 23048 | tf_op jit(solution)/shard_map/ppermute | solution.py:28
  44.3 8.8 %collective-permute-start.5 = (f32[5,3,1,128]{3,2,1,0:T(1,128)S(1)}, f32[5,3,1,128]{3,2,1,0:T(1,128)S(1)}, u32[]{:S(2)}, u32[]{:S(2)}) collective-permute-start(f32[5,3,1,128]{3,2,1,0:T(1,128)S(1)} %pad_maximum_fusion.6), channel_id=1, source_target_pairs={{0,1},{1,2},{2,3},{4,5},{5,6},{6,7},{8,9},{9,10},{10,11},{12,13},{... | collective-permute-start | bytes 23048 | tf_op jit(solution)/shard_map/ppermute | solution.py:27
  47.4 6.5 %collective-permute-start.6 = (f32[16,3,1,128]{3,0,2,1:T(8,128)S(1)}, f32[16,3,1,128]{3,0,2,1:T(8,128)S(1)}, u32[]{:S(2)}, u32[]{:S(2)}) collective-permute-start(f32[16,3,1,128]{3,0,2,1:T(8,128)S(1)} %pad_maximum_fusion), channel_id=1, source_target_pairs={{1,0},{2,1},{3,2},{5,4},{6,5},{7,6},{9,8},{10,9},{11,10},{13,12},{... | collective-permute-start | bytes 73736 | tf_op jit(solution)/shard_map/ppermute | solution.py:28
  48.7 4.5 %collective-permute-start.2 = (f32[16,3,1,128]{3,0,2,1:T(8,128)S(1)}, f32[16,3,1,128]{3,0,2,1:T(8,128)S(1)}, u32[]{:S(2)}, u32[]{:S(2)}) collective-permute-start(f32[16,3,1,128]{3,0,2,1:T(8,128)S(1)} %pad_maximum_fusion), channel_id=1, source_target_pairs={{0,1},{1,2},{2,3},{4,5},{5,6},{6,7},{8,9},{9,10},{10,11},{12,13},{... | collective-permute-start | bytes 73736 | tf_op jit(solution)/shard_map/ppermute | solution.py:27
  87.9 2.9 %collective-permute-start.8 = (f32[16,1,1,128]{3,0,2,1:T(8,128)S(1)}, f32[16,1,1,128]{3,0,2,1:T(8,128)S(1)}, u32[]{:S(2)}, u32[]{:S(2)}) collective-permute-start(f32[16,1,1,128]{3,0,2,1:T(8,128)S(1)} %bitcast.216), channel_id=1, source_target_pairs={{0,4},{4,8},{8,12},{1,5},{5,9},{9,13},{2,6},{6,10},{10,14},{3,7},{... | collective-permute-start | bytes 24584 | tf_op jit(solution)/shard_map/ppermute | solution.py:27
  89.2 5.5 %collective-permute-start.9 = (f32[16,1,1,128]{3,0,2,1:T(8,128)S(1)}, f32[16,1,1,128]{3,0,2,1:T(8,128)S(1)}, u32[]{:S(2)}, u32[]{:S(2)}) collective-permute-start(f32[16,1,1,128]{3,0,2,1:T(8,128)S(1)} %bitcast.217), channel_id=1, source_target_pairs={{4,0},{8,4},{12,8},{5,1},{9,5},{13,9},{6,2},{10,6},{14,10},{7,3},{... | collective-permute-start | bytes 24584 | tf_op jit(solution)/shard_map/ppermute | solution.py:28
  94.8 5.8 %collective-permute-start.11 = (f32[16,3,1,128]{3,0,2,1:T(8,128)S(1)}, f32[16,3,1,128]{3,0,2,1:T(8,128)S(1)}, u32[]{:S(2)}, u32[]{:S(2)}) collective-permute-start(f32[16,3,1,128]{3,0,2,1:T(8,128)S(1)} %pad_maximum_fusion.1), channel_id=1, source_target_pairs={{1,0},{2,1},{3,2},{5,4},{6,5},{7,6},{9,8},{10,9},{11,10},{13,12},{... | collective-permute-start | bytes 73736 | tf_op jit(solution)/shard_map/ppermute | solution.py:28
  96.1 3.9 %collective-permute-start.10 = (f32[16,3,1,128]{3,0,2,1:T(8,128)S(1)}, f32[16,3,1,128]{3,0,2,1:T(8,128)S(1)}, u32[]{:S(2)}, u32[]{:S(2)}) collective-permute-start(f32[16,3,1,128]{3,0,2,1:T(8,128)S(1)} %pad_maximum_fusion.1), channel_id=1, source_target_pairs={{0,1},{1,2},{2,3},{4,5},{5,6},{6,7},{8,9},{9,10},{10,11},{12,13},{... | collective-permute-start | bytes 73736 | tf_op jit(solution)/shard_map/ppermute | solution.py:27
